TPU v7x, 768 devices: a whole 4x8x12 slice. The times are simulated.
768 devices in a mesh: win: 192 (over y, z_lo, x), tok: 4 (over z_hi, core).
Axes of the slice: x: 4, y: 8, z: 12 (z_hi: 2, z_lo: 6; z = z_hi * 6 + z_lo), core: 2. Of those that a mesh axis runs over, the one named last changes fastest.
Arguments:
- field_tokens: bfloat16 [192, 40, 40, 1280], P('win', 'tok'), may hold values from -60 to 60
- lon_shift: int32 [4], replicated, may hold values from 1 to 20, as said below
- norm_gain: float32 [1280], replicated, may hold values from 0.1 to 1.9
- qkv_weight: bfloat16 [1280, 1920], replicated, may hold values from -1 to 1
- out_weight: bfloat16 [640, 1280], replicated, may hold values from -0.25 to 0.25
Outputs:
- result: bfloat16 [192, 40, 40, 1280], P('win', 'tok')
Inputs may be any that keep to these rules, and one draw needn't show every extreme that they name: `lon_shift`: one entry is 20 and another is 1.
All inputs are finite; a program needn't handle non-finite values.
Results may differ from a plain program's by a relative error of at most 0.0046.
Values may be sent and summed in bfloat16 or wider, within the bound.
A program may use at most 64 MiB of HBM per device.

v0:
```python
import jax
import jax.numpy as jnp
from jax import lax
from jax.sharding import PartitionSpec as P

HEADS = 8
HD = 80
LAT_WINDOWS = 4


def shifted(block, axis, distance):
    devices = range(lax.axis_size(axis))
    route = [((i - distance) % len(devices), i) for i in devices]
    return lax.ppermute(block, axis, route)


def attend(packed):
    queries = packed[:, 0, 0]
    key_rows = packed[:, 1, 0]
    value_rows = packed[:, 2, 0]
    count = queries.shape[0]
    local_heads = queries.shape[1]
    head_size = queries.shape[2]
    factor = head_size ** (-0.5)
    pieces = 2
    grouped = queries.reshape(pieces, count // pieces, local_heads, head_size)

    def one_block(query_block):
        scores = (
            jnp.einsum("qhd,khd->hqk", query_block, key_rows, preferred_element_type=jnp.float32)
            * factor
        )
        row_top = jnp.max(scores, axis=-1, keepdims=True)
        exponent = jnp.exp(scores - row_top)
        weights = (exponent / jnp.sum(exponent, axis=-1, keepdims=True)).astype(jnp.bfloat16)
        return jnp.einsum(
            "hqk,khd->qhd", weights, value_rows, preferred_element_type=jnp.float32
        ).astype(jnp.bfloat16)

    return lax.map(one_block, grouped).reshape(count, local_heads, head_size)


def shards(field_tokens, lon_shift, norm_gain, qkv_weight, out_weight):
    row_count = field_tokens.shape[1]
    column_count = field_tokens.shape[2]
    feature_count = field_tokens.shape[3]
    groups = lax.axis_size("tok")
    latitude = lax.axis_index("win") % LAT_WINDOWS
    offset = lax.dynamic_index_in_dim(lon_shift, latitude, 0, keepdims=False)
    eastern = shifted(field_tokens, "win", -LAT_WINDOWS)
    joined = jnp.concatenate([field_tokens, eastern], axis=2)
    moved = lax.dynamic_slice_in_dim(joined, offset, column_count, axis=2)
    tokens = moved.reshape(row_count * column_count, feature_count)
    values = tokens.astype(jnp.float32)
    factor = lax.rsqrt(jnp.mean(values * values, axis=-1, keepdims=True) + 1e-06)
    normed = (values * factor * norm_gain).astype(jnp.bfloat16)
    qkv = jnp.dot(normed, qkv_weight, preferred_element_type=jnp.float32).astype(jnp.bfloat16)
    qkv = qkv.reshape(row_count * column_count, 3, groups, HEADS // groups, HD)
    attended = attend(lax.all_to_all(qkv, "tok", split_axis=2, concat_axis=0, tiled=True))
    returned = lax.all_to_all(attended, "tok", split_axis=0, concat_axis=1, tiled=True)
    projected = jnp.dot(
        returned.reshape(row_count * column_count, HEADS * HD),
        out_weight,
        preferred_element_type=jnp.float32,
    )
    mixed = (
        (values + projected).astype(jnp.bfloat16).reshape(1, row_count, column_count, feature_count)
    )
    western = shifted(mixed, "win", LAT_WINDOWS)
    combined = jnp.concatenate([western, mixed], axis=2)
    return lax.dynamic_slice_in_dim(combined, western.shape[2] - offset, column_count, axis=2)


def solution(mesh):
    placed = (P("win", "tok", None, None), P(), P(), P(), P())
    return jax.shard_map(
        shards, mesh=mesh, in_specs=placed, out_specs=P("win", "tok", None, None), check_vma=False
    )
```

profile of v0, /device:TPU:6, one launch (start us, length us, event | category | flops | bytes accessed | tf_op | source)
XLA Modules:
  0.0 249.8 jit_solution(3299379259092738246)
XLA Ops:
  0.0 0.0 copy-start
  0.0 15.8 %collective-permute-start = (bf16[1,10,40,1280]{3,2,1,0:T(8,128)(2,1)}, bf16[1,10,40,1280]{3,2,1,0:T(8,128)(2,1)S(1)}, u32[]{:S(2)}, u32[]{:S(2)}) collective-permute-start(bf16[1,10,40,1280]{3,2,1,0:T(8,128)(2,1)} %param.7), channel_id=1, source_target_pairs={{16,0},{20,4},{24,8},{28,12},{32,16},{36,20},{40,24},{44,28},{48,3... | collective-permute-start | bytes 3072008 | tf_op jit(solution)/shard_map/ppermute | solution.py:14
  15.8 1.3 dynamic_slice.14
  19.2 0.0 copy-start.3
  19.2 18.7 %collective-permute-done = bf16[1,10,40,1280]{3,2,1,0:T(8,128)(2,1)S(1)} collective-permute-done((bf16[1,10,40,1280]{3,2,1,0:T(8,128)(2,1)}, bf16[1,10,40,1280]{3,2,1,0:T(8,128)(2,1)S(1)}, u32[]{:S(2)}, u32[]{:S(2)}) %collective-permute-start) | collective-permute-done | bytes 1024032 | tf_op jit(solution)/shard_map/ppermute | solution.py:14
  37.9 3.3 %multiply_reduce_fusion.1 = (f32[10,40]{1,0:T(8,128)S(1)}, f32[1,10,40,1280]{3,2,1,0:T(8,128)}) fusion(s32[]{:T(128)S(6)} %select_n.19, bf16[1,10,40,1280]{3,2,1,0:T(8,128)(2,1)S(1)} %collective-permute-done, bf16[1,10,40,1280]{3,2,1,0:T(8,128)(2,1)} %param.7), kind=kLoop, calls=%fused_computation.29 | loop fusion | flops 3071600 | bytes 4097604 | tf_op jit(solution)/shard_map/reduce_sum | solution.py:55
  41.3 0.1 rsqrt.12
  41.4 0.0 copy-done.3
  41.4 1.8 fusion.29
  43.2 4.7 %convolution_convert_fusion = bf16[400,1920]{1,0:T(8,128)(2,1)S(1)} fusion(bf16[400,1280]{1,0:T(8,128)(2,1)S(1)} %fusion.29, bf16[1280,1920]{1,0:T(8,128)(2,1)} %param.10), kind=kOutput, calls=%fused_computation.21 | convolution fusion | flops 1966848000 | bytes 7475200 | tf_op jit(solution)/shard_map/dot_general | solution.py:57
  47.9 2.3 copy.16
  50.2 3.0 %copy.17 = bf16[400,3,4,2,80]{0,4,3,1,2:T(8,128)(2,1)} copy(bf16[400,3,4,2,80]{0,4,3,2,1:T(8,128)(2,1)} %bitcast.62) | data formatting | bytes 3072000 | tf_op jit(solution)/shard_map/reshape | solution.py:58
  53.2 9.4 %all-to-all-start = ((bf16[400,3,4,2,80]{0,4,3,1,2:T(8,128)(2,1)}), bf16[400,3,4,2,80]{0,4,3,1,2:T(8,128)(2,1)}, u32[]{:S(2)}, u32[]{:S(2)}) async-start(bf16[400,3,4,2,80]{0,4,3,1,2:T(8,128)(2,1)} %copy.17), calls=%async_computation | async-start | bytes 3932160 | tf_op jit(solution)/shard_map/all_to_all | solution.py:59
  62.6 66.2 %all-to-all-done = bf16[400,3,4,2,80]{0,4,3,1,2:T(8,128)(2,1)} async-done(((bf16[400,3,4,2,80]{0,4,3,1,2:T(8,128)(2,1)}), bf16[400,3,4,2,80]{0,4,3,1,2:T(8,128)(2,1)}, u32[]{:S(2)}, u32[]{:S(2)}) %all-to-all-start) | async-done | bytes 1536032 | tf_op jit(solution)/shard_map/all_to_all | solution.py:59
  128.8 4.3 %copy.18 = bf16[4,400,3,1,2,80]{1,0,5,4,2,3:T(4,128)(2,1)} copy(bf16[4,400,3,1,2,80]{1,5,4,2,0,3:T(8,128)(2,1)} %bitcast.7) | data formatting | bytes 3072000 | tf_op jit(solution)/shard_map/all_to_all | solution.py:59
  133.1 3.9 %all_to_all.27 = bf16[1600,3,1,2,80]{0,4,3,1,2:T(8,128)(2,1)S(1)} reshape(bf16[4,400,3,1,2,80]{1,0,5,4,2,3:T(4,128)(2,1)} %copy.18) | data formatting | bytes 3072000 | tf_op jit(solution)/shard_map/all_to_all | solution.py:59
  137.0 1.3 slice_bitcast_fusion
  138.3 0.0 copy-start.1
  138.3 2.2 reshape_squeeze.3
  140.5 0.1 copy.19
  140.6 0.0 copy-done.1
  140.6 29.0 %while.10 = (s32[]{:T(128)}, bf16[2,800,2,80]{1,3,2,0:T(8,128)(2,1)S(1)}, bf16[2,800,2,80]{1,3,2,0:T(8,128)(2,1)S(1)}, bf16[1600,2,80]{0,2,1:T(8,128)(2,1)}, bf16[1600,2,80]{0,2,1:T(8,128)(2,1)}, /*index=5*/s32[]{:T(128)}) while((s32[]{:T(128)}, bf16[2,800,2,80]{1,3,2,0:T(8,128)(2,1)S(1)}, bf16[2,800,2,80]{1,3,2,0:T(8,128)(2,1)S(1)}, ...), condition=%wide.region_4.5_spmd, body=%wide.region_1.4_spmd.sunk | while | flops 832129600 | bytes 24159592 | solution.py:40
  140.6 0.0 copy-start.2
  140.6 8.6 %fusion.54 = (f32[2,800]{1,0:T(2,128)S(1)}, f32[2,800,1600]{2,1,0:T(8,128)}) fusion(bf16[1600,2,80]{0,2,1:T(8,128)(2,1)} %get-tuple-element.115, bf16[2,800,2,80]{1,3,2,0:T(8,128)(2,1)S(1)} %get-tuple-element.114, s32[]{:T(128)} %get-tuple-element.106), kind=kOutput, calls=%fused_computation.36.clone.1 | convolution fusion | flops 417281600 | bytes 11045124 | tf_op jit(solution)/shard_map/while/body/eval_jaxpr/sub | solution.py:34
  149.2 0.0 copy-done.2
  149.2 5.9 %fusion.55 = bf16[2,800,2,80]{1,3,2,0:T(8,128)(2,1)S(1)} fusion(bf16[2,800,2,80]{1,3,2,0:T(8,128)(2,1)S(1)} %get-tuple-element.107, s32[]{:T(128)} %get-tuple-element.106, bf16[1600,2,80]{0,2,1:T(8,128)(2,1)S(1)} %copy-done.2, f32[2,800,1600]{2,1,0:T(8,128)} %get-tuple-element.98, f32[2,800]{1,0:T(2,128)S(1)} %get-tuple-element.99), kind=kOutput, calls=%fused_computation.10.clone.1 | convolution fusion | flops 414848000 | bytes 11066372 | tf_op jit(solution)/shard_map/while/body/eval_jaxpr/hqk,khd->qhd/dot_general | solution.py:36
  155.1 0.0 copy-start.2
  155.1 8.6 %fusion.54 = (f32[2,800]{1,0:T(2,128)S(1)}, f32[2,800,1600]{2,1,0:T(8,128)}) fusion(bf16[1600,2,80]{0,2,1:T(8,128)(2,1)} %get-tuple-element.115, bf16[2,800,2,80]{1,3,2,0:T(8,128)(2,1)S(1)} %get-tuple-element.114, s32[]{:T(128)} %get-tuple-element.106), kind=kOutput, calls=%fused_computation.36.clone.1 | convolution fusion | flops 417281600 | bytes 11045124 | tf_op jit(solution)/shard_map/while/body/eval_jaxpr/sub | solution.py:34
  163.7 0.0 copy-done.2
  163.7 5.9 %fusion.55 = bf16[2,800,2,80]{1,3,2,0:T(8,128)(2,1)S(1)} fusion(bf16[2,800,2,80]{1,3,2,0:T(8,128)(2,1)S(1)} %get-tuple-element.107, s32[]{:T(128)} %get-tuple-element.106, bf16[1600,2,80]{0,2,1:T(8,128)(2,1)S(1)} %copy-done.2, f32[2,800,1600]{2,1,0:T(8,128)} %get-tuple-element.98, f32[2,800]{1,0:T(2,128)S(1)} %get-tuple-element.99), kind=kOutput, calls=%fused_computation.10.clone.1 | convolution fusion | flops 414848000 | bytes 11066372 | tf_op jit(solution)/shard_map/while/body/eval_jaxpr/hqk,khd->qhd/dot_general | solution.py:36
  169.6 1.4 copy.23
  171.0 38.3 %all_to_all.33 = bf16[1600,2,80]{2,1,0:T(2,128)(2,1)S(1)} all-to-all(bf16[1600,2,80]{2,1,0:T(2,128)(2,1)S(1)} %bitcast.63), channel_id=1, replica_groups=mesh['win'=192,'tok'=4] {'tok'}, dimensions={0} | all-to-all | bytes 1024000 | tf_op jit(solution)/shard_map/all_to_all | solution.py:60
  209.3 1.8 copy.22
  211.2 0.0 copy-done
  211.2 2.8 %fusion.27 = bf16[400,1280]{1,0:T(8,128)(2,1)S(1)} fusion(f32[400,1280]{1,0:T(8,128)} %bitcast.61, bf16[400,640]{0,1:T(8,128)(2,1)} %bitcast.67, bf16[640,1280]{1,0:T(8,128)(2,1)S(1)} %copy-done), kind=kOutput, calls=%fused_computation.20 | convolution fusion | flops 656384000 | bytes 5222400 | tf_op jit(solution)/shard_map/dot_general | solution.py:61
  214.0 1.9 collective-permute-start.1
  217.3 29.9 %collective-permute-done.1 = bf16[1,10,40,1280]{3,2,1,0:T(8,128)(2,1)} collective-permute-done((bf16[1,10,40,1280]{3,2,1,0:T(8,128)(2,1)S(1)}, bf16[1,10,40,1280]{3,2,1,0:T(8,128)(2,1)}, u32[]{:S(2)}, u32[]{:S(2)}) %collective-permute-start.1) | collective-permute-done | bytes 1024032 | tf_op jit(solution)/shard_map/ppermute | solution.py:14
  247.2 2.6 %fusion.30 = bf16[1,10,40,1280]{3,2,1,0:T(8,128)(2,1)} fusion(s32[]{:T(128)S(6)} %select_n.20, bf16[1,10,40,1280]{3,2,1,0:T(8,128)(2,1)} %collective-permute-done.1, bf16[1,10,40,1280]{3,2,1,0:T(8,128)(2,1)S(1)} %bitcast.66), kind=kLoop, calls=%fused_computation.30 | loop fusion | flops 2048000 | bytes 3072004 | tf_op jit(solution)/shard_map/concatenate | solution.py:70
  (2 shorter events, 0.0 us)
Async XLA Ops:
  0.0 211.2 %copy-start = (bf16[640,1280]{1,0:T(8,128)(2,1)S(1)}, bf16[640,1280]{1,0:T(8,128)(2,1)}, u32[]{:S(2)}) copy-start(bf16[640,1280]{1,0:T(8,128)(2,1)} %param.11) | copy-start | bytes 4915204
  0.0 37.9 %collective-permute-start = (bf16[1,10,40,1280]{3,2,1,0:T(8,128)(2,1)}, bf16[1,10,40,1280]{3,2,1,0:T(8,128)(2,1)S(1)}, u32[]{:S(2)}, u32[]{:S(2)}) collective-permute-start(bf16[1,10,40,1280]{3,2,1,0:T(8,128)(2,1)} %param.7), channel_id=1, source_target_pairs={{16,0},{20,4},{24,8},{28,12},{32,16},{36,20},{40,24},{44,28},{48,3... | collective-permute-start | bytes 3072008 | tf_op jit(solution)/shard_map/ppermute | solution.py:14
  19.2 22.2 %copy-start.3 = (f32[1280]{0:T(1024)S(1)}, f32[1280]{0:T(1024)}, u32[]{:S(2)}) copy-start(f32[1280]{0:T(1024)} %param.9) | copy-start | bytes 15364
  53.2 75.6 %all-to-all-start = ((bf16[400,3,4,2,80]{0,4,3,1,2:T(8,128)(2,1)}), bf16[400,3,4,2,80]{0,4,3,1,2:T(8,128)(2,1)}, u32[]{:S(2)}, u32[]{:S(2)}) async-start(bf16[400,3,4,2,80]{0,4,3,1,2:T(8,128)(2,1)} %copy.17), calls=%async_computation | async-start | bytes 3932160 | tf_op jit(solution)/shard_map/all_to_all | solution.py:59
  138.3 2.3 copy-start.1
  140.6 8.6 %copy-start.2 = (bf16[1600,2,80]{0,2,1:T(8,128)(2,1)S(1)}, bf16[1600,2,80]{0,2,1:T(8,128)(2,1)}, u32[]{:S(2)}) copy-start(bf16[1600,2,80]{0,2,1:T(8,128)(2,1)} %get-tuple-element.116) | copy-start | bytes 1536004 | tf_op jit(solution)/shard_map/while
  155.1 8.6 %copy-start.2 = (bf16[1600,2,80]{0,2,1:T(8,128)(2,1)S(1)}, bf16[1600,2,80]{0,2,1:T(8,128)(2,1)}, u32[]{:S(2)}) copy-start(bf16[1600,2,80]{0,2,1:T(8,128)(2,1)} %get-tuple-element.116) | copy-start | bytes 1536004 | tf_op jit(solution)/shard_map/while
  214.0 33.2 %collective-permute-start.1 = (bf16[1,10,40,1280]{3,2,1,0:T(8,128)(2,1)S(1)}, bf16[1,10,40,1280]{3,2,1,0:T(8,128)(2,1)}, u32[]{:S(2)}, u32[]{:S(2)}) collective-permute-start(bf16[1,10,40,1280]{3,2,1,0:T(8,128)(2,1)S(1)} %bitcast.65), channel_id=1, source_target_pairs={{752,0},{756,4},{760,8},{764,12},{0,16},{4,20},{8,24},{12,28},{16,... | collective-permute-start | bytes 3072008 | tf_op jit(solution)/shard_map/ppermute | solution.py:14
where the time goes:
time: 251 us; the launch traced here: 250 us
  waiting for transfers between devices  115 us (46%)
  blocking collectives  38.3 us (15%)
  matrix products  36.4 us (15%)
  starting transfers between devices  27.1 us (11%)
  local copies, waits for them, and re-layouts  21.7 us (9%)
  other arithmetic  7.74 us (3%)
  between operations  3.6 us (1%)
    all_to_all x1, waiting for transfers between devices, shards(): lax.all_to_all(qkv, 'tok', split_axis=2, concat_axis=0, tiled=True)  66.2 us
    ppermute x2, waiting for transfers between devices, shifted(): return lax.ppermute(block, axis, route)  48.7 us
    all_to_all x1, blocking collectives, shards(): lax.all_to_all(attended, 'tok', split_axis=0, concat_axis=1, tiled=True)  38.3 us
    ppermute x2, starting transfers between devices, shifted(): return lax.ppermute(block, axis, route)  17.7 us
    sub x2, matrix products, one_block(): exponent = jnp.exp(scores - row_top)  17.2 us
    dot_general x2, matrix products, one_block(): jnp.einsum('hqk,khd->qhd', weights, value_rows, preferred_element_type=jn...  11.7 us
    all_to_all x1, starting transfers between devices, shards(): lax.all_to_all(qkv, 'tok', split_axis=2, concat_axis=0, tiled=True)  9.4 us
    all_to_all x2, local copies, waits for them, and re-layouts, shards(): lax.all_to_all(qkv, 'tok', split_axis=2, concat_axis=0, tiled=True)  8.23 us
  transfers between devices with their start and end apart: 3, of which 3 were waited for; matrix products, arithmetic and copies ran while one was open for 1% of the time, Pallas kernels for 0%

commit v1 on v0

v1 whole, which is shorter than its diff:
```python
import functools

import jax
import jax.numpy as jnp
from jax import lax
from jax.experimental import pallas as pl
from jax.experimental.pallas import tpu as pltpu
from jax.sharding import PartitionSpec as P

HEADS = 8
HD = 80
LAT_WINDOWS = 4
ZLO = 6
ROWS = 10
COLS = 40
D = 1280
WIDTH = HEADS * HD
EAST = 24
REST = COLS - EAST
NM = ROWS * EAST
NO = ROWS * REST
NT = NM + NO
GROUP = 4
QW = 384
QB = 160
MESH = pl.DeviceIdType.MESH
CHUNKS = ((0, 256), (256, 128), (384, 128), (512, 128))
RETURNS = ((0, 256), (256, 128))
F32 = jnp.float32
BF16 = jnp.bfloat16


def kernel(
    shift_ref, gain_ref, x_hbm, w_hbm, wo_hbm, out_ref,
    xv, xe, wv, wo, nb, kv, kvo, qa, qs, pb, lb, ao, ai, rt,
    load_sem, shift_s, shift_r, ko_s, ko_r, km_s, km_r, sib_s, sib_r, ret_s, ret_r,
):
    win, tok = lax.axis_index("win"), lax.axis_index("tok")
    n_win = 192
    core = tok % 2
    half = tok // 2
    other = 1 - core
    sib = (win, half * 2 + other)
    anti = ((win, (1 - half) * 2), (win, (1 - half) * 2 + 1))
    east_w = (win + LAT_WINDOWS) % n_win
    west_w = (win + n_win - LAT_WINDOWS) % n_win
    east, east_sib = (east_w, tok), (east_w, half * 2 + other)
    west, west_sib = (west_w, tok), (west_w, half * 2 + other)

    loads = [
        pltpu.make_async_copy(x_hbm.at[0], xv, load_sem.at[0]),
        pltpu.make_async_copy(w_hbm, wv, load_sem.at[1]),
        pltpu.make_async_copy(wo_hbm.at[pl.ds(0, 320)], wo.at[0, pl.ds(64, 320)], load_sem.at[2]),
        pltpu.make_async_copy(wo_hbm.at[pl.ds(320, 320)], wo.at[1, pl.ds(64, 320)], load_sem.at[3]),
    ]
    for c in loads:
        c.start()

    barrier = pltpu.get_barrier_semaphore()
    peers = (east, east_sib, west, west_sib, sib, anti[0], anti[1])
    for d in peers:
        pl.semaphore_signal(barrier, inc=1, device_id=d, device_id_type=MESH)
    wo[:, 0:64, :] = jnp.zeros((2, 64, D), BF16)
    pl.semaphore_wait(barrier, len(peers))

    def remote(src, dst, s, r, d):
        return pltpu.make_async_remote_copy(
            src_ref=src, dst_ref=dst, send_sem=s, recv_sem=r, device_id=d, device_id_type=MESH
        )

    shift = remote(x_hbm.at[0, :, pl.ds(0, EAST), :], xe, shift_s, shift_r, west)
    shift.start()

    offset = shift_ref[win % LAT_WINDOWS]
    gain = gain_ref[...]

    def project(values, row0, count):
        factor = lax.rsqrt(jnp.mean(values * values, axis=-1, keepdims=True) + 1e-06)
        nb[pl.ds(0, count), :] = (values * factor * gain).astype(BF16)
        normed = nb[pl.ds(0, count), :]
        rows = pl.ds(row0, count)

        def part(i):
            return jnp.dot(normed, wv[:, i * WIDTH : (i + 1) * WIDTH], preferred_element_type=F32)

        lane = lax.broadcasted_iota(jnp.int32, (count, 128), 1)
        low = lane < 64
        k = part(1)
        v = part(2)
        rk = pltpu.roll(k[:, 256:640], 320, 1)
        rv = pltpu.roll(v[:, 0:384], 64, 1)
        g0 = [k[:, 0:256], jnp.where(low, k[:, 256:384], rv[:, 0:128]), rv[:, 128:384]]
        g1 = [rk[:, 0:256], jnp.where(low, rk[:, 256:384], v[:, 256:384]), v[:, 384:640]]
        lanes = ((0, 256), (256, 384), (384, 640))
        first = core == 0
        for (a, b), u0, u1 in zip(lanes, g0, g1):
            kvo[0, rows, a:b] = u0.astype(BF16)
            kvo[1, rows, a:b] = u1.astype(BF16)
            kv[0, rows, a:b] = jnp.where(first, u0, u1).astype(BF16)
        q = part(0)
        q0 = q[:, 0:384]
        q1 = pltpu.roll(q[:, 256:640], 320, 1)
        qa[rows, :] = jnp.where(first, q0, q1).astype(BF16)
        qs[rows, :] = jnp.where(first, q1, q0).astype(BF16)

    loads[0].wait()
    own_rest = xv[:, EAST:COLS, :].astype(F32).reshape(NO, D)
    loads[1].wait()
    project(own_rest, NM, NO)
    tail, sib_tail = pl.ds(NM, NO), pl.ds(NT + NM, NO)
    head, sib_head = pl.ds(0, NM), pl.ds(NT, NM)
    sib_all = pl.ds(NT, NT)
    sends = [shift]
    ko = [
        remote(kvo.at[g, tail, :], kv.at[2 + core, tail, :], ko_s.at[g], ko_r.at[core], anti[g])
        for g in range(2)
    ]
    sib_o = [
        remote(kvo.at[other, tail, :], kv.at[1, tail, :], sib_s.at[0], sib_r.at[0], sib),
        remote(qs.at[tail, :], qa.at[sib_tail, :], sib_s.at[1], sib_r.at[1], sib),
    ]
    for c in ko + sib_o:
        c.start()
    sends += ko + sib_o

    column = lax.broadcasted_iota(jnp.int32, (ROWS, EAST, 1), 1)
    from_east = column < offset
    own_east = xv[:, 0:EAST, :].astype(F32)
    shift.wait_recv()
    mixed = jnp.where(from_east, xe[...].astype(F32), own_east).reshape(NM, D)
    project(mixed, 0, NM)
    sib_m = [
        remote(kvo.at[other, head, :], kv.at[1, head, :], sib_s.at[2], sib_r.at[2], sib),
        remote(qs.at[head, :], qa.at[sib_head, :], sib_s.at[3], sib_r.at[3], sib),
    ]
    km = []
    for i, (a, n) in enumerate(CHUNKS):
        for g in range(2):
            km.append(
                remote(
                    kvo.at[g, head, pl.ds(a, n)], kv.at[2 + core, head, pl.ds(a, n)],
                    km_s.at[i, g], km_r.at[i, core], anti[g],
                )
            )
    for c in km + sib_m:
        c.start()
    sends += km + sib_m

    for c in sib_o + sib_m:
        c.wait_recv()
    for s in range(2):
        remote(kvo.at[0, tail, :], kv.at[2 + s, tail, :], ko_s.at[0], ko_r.at[s], anti[0]).wait_recv()

    def arrived(i):
        a, n = CHUNKS[i]
        for s in range(2):
            remote(
                kvo.at[0, head, pl.ds(a, n)], kv.at[2 + s, head, pl.ds(a, n)],
                km_s.at[i, 0], km_r.at[i, s], anti[0],
            ).wait_recv()

    scale = HD ** (-0.5) * 1.4426950408889634

    def scores(h):
        a = (80 * h) // 128 * 128
        b = (80 * h + 79) // 128 * 128 + 128
        lane = lax.broadcasted_iota(jnp.int32, (QB, b - a), 1) + a
        keep = (lane >= 80 * h) & (lane < 80 * h + 80)
        keys = kv.at[:, :, pl.ds(a, b - a)]

        @pl.loop(0, 2 * NT // QB)
        def _(i):
            rows = pl.ds(pl.multiple_of(i * QB, QB), QB)
            q = jnp.where(keep, qa[rows, a:b].astype(F32), 0.0).astype(BF16)
            s = lax.dot_general(
                q, keys[...].reshape(4 * NT, b - a), (((1,), (1,)), ((), ())), preferred_element_type=F32
            )
            top = jnp.max(s, axis=-1, keepdims=True)
            e = jnp.exp2((s - top) * scale)
            lb[h, rows, :] = 1.0 / jnp.sum(e, axis=-1, keepdims=True)
            pb[h, rows, :] = e.astype(BF16)

    def values(lanes, heads):
        a, n = lanes
        lane = lax.broadcasted_iota(jnp.int32, (QB, n), 1) + a

        @pl.loop(0, 2 * NT // QB)
        def _(i):
            rows = pl.ds(pl.multiple_of(i * QB, QB), QB)
            total = jnp.zeros((QB, n), F32)
            vals = kv[:, :, 256 + a : 256 + a + n].reshape(4 * NT, n)
            for h in heads:
                o = jnp.dot(pb[h, rows, :], vals, preferred_element_type=F32) * lb[h, rows, :]
                first = 64 + 80 * h
                total = jnp.where((lane >= first) & (lane < first + 80), o, total)
            ao[rows, a : a + n] = total.astype(BF16)

    arrived(0)
    scores(0)
    scores(1)
    scores(2)
    arrived(1)
    scores(3)
    arrived(2)
    back = []

    def give(i):
        a, n = RETURNS[i]
        l = pl.ds(a, n)
        cs = [
            remote(ao.at[head, l], rt.at[core, :, l], ret_s.at[i, 0], ret_r.at[i, core], east),
            remote(ao.at[sib_head, l], rt.at[core, :, l], ret_s.at[i, 1], ret_r.at[i, core], east_sib),
            remote(ao.at[sib_all, l], ai.at[:, l], ret_s.at[i, 2], ret_r.at[i, 2], sib),
        ]
        for c in cs:
            c.start()
        return cs

    values((0, 256), (0, 1, 2))
    sends += give(0)
    arrived(3)
    values((256, 128), (2, 3))
    sends += give(1)

    loads[2].wait()
    loads[3].wait()

    for i, (a, n) in enumerate(RETURNS):
        l = pl.ds(a, n)
        remote(ao.at[sib_all, l], ai.at[:, l], ret_s.at[i, 2], ret_r.at[i, 2], sib).wait_recv()
    rest = jnp.dot(ao[NM:NT, :], wo[core], preferred_element_type=F32)
    rest += jnp.dot(ai[NM:NT, :], wo[other], preferred_element_type=F32)
    own_rest = xv[:, EAST:COLS, :].astype(F32)
    out_ref[0, :, EAST:COLS, :] = (own_rest + rest.reshape(ROWS, REST, D)).astype(BF16)

    for i, (a, n) in enumerate(RETURNS):
        l = pl.ds(a, n)
        for s in range(2):
            remote(ao.at[head, l], rt.at[s, :, l], ret_s.at[i, 0], ret_r.at[i, s], east).wait_recv()
    away = from_east

    def pick(far, near):
        far3 = far.astype(F32).reshape(ROWS, EAST, QW)
        near3 = near.astype(F32).reshape(ROWS, EAST, QW)
        return jnp.where(away, far3, near3).reshape(NM, QW).astype(BF16)

    moved = jnp.dot(pick(rt[core], ao[0:NM, :]), wo[core], preferred_element_type=F32)
    moved += jnp.dot(pick(rt[other], ai[0:NM, :]), wo[other], preferred_element_type=F32)
    own_east = xv[:, 0:EAST, :].astype(F32)
    out_ref[0, :, 0:EAST, :] = (own_east + moved.reshape(ROWS, EAST, D)).astype(BF16)

    for c in sends:
        c.wait_send()


def shards(field_tokens, lon_shift, norm_gain, qkv_weight, out_weight):
    any_spec = pl.BlockSpec(memory_space=pl.ANY)
    dma = pltpu.SemaphoreType.DMA
    return pl.pallas_call(
        kernel,
        out_shape=jax.ShapeDtypeStruct((1, ROWS, COLS, D), BF16),
        in_specs=[
            pl.BlockSpec(memory_space=pltpu.SMEM),
            pl.BlockSpec(memory_space=pltpu.VMEM),
            any_spec, any_spec, any_spec,
        ],
        out_specs=pl.BlockSpec(memory_space=pltpu.VMEM),
        scratch_shapes=[
            pltpu.VMEM((ROWS, COLS, D), BF16),
            pltpu.VMEM((ROWS, EAST, D), BF16),
            pltpu.VMEM((D, 3 * WIDTH), BF16),
            pltpu.VMEM((2, QW, D), BF16),
            pltpu.VMEM((NM, D), BF16),
            pltpu.VMEM((4, NT, WIDTH), BF16),
            pltpu.VMEM((2, NT, WIDTH), BF16),
            pltpu.VMEM((2 * NT, QW), BF16),
            pltpu.VMEM((NT, QW), BF16),
            pltpu.VMEM((GROUP, 2 * NT, 4 * NT), BF16),
            pltpu.VMEM((GROUP, 2 * NT, 1), F32),
            pltpu.VMEM((2 * NT, QW), BF16),
            pltpu.VMEM((NT, QW), BF16),
            pltpu.VMEM((2, NM, QW), BF16),
            dma((4,)),
            dma(()), dma(()),
            dma((2,)), dma((2,)),
            dma((4, 2)), dma((4, 2)),
            dma((4,)), dma((4,)),
            dma((2, 3)), dma((2, 3)),
        ],
        name="window_attention",
        compiler_params=pltpu.CompilerParams(collective_id=0, has_side_effects=True),
    )(lon_shift, norm_gain.reshape(1, D), field_tokens, qkv_weight, out_weight)


def solution(mesh):
    placed = (P("win", "tok", None, None), P(), P(), P(), P())
    return jax.shard_map(
        shards, mesh=mesh, in_specs=placed, out_specs=P("win", "tok", None, None), check_vma=False
    )
```

time: 251 us -> 124 us (0.49)
  the two profiles are of different devices: /device:TPU:6 before, /device:TPU:50 now
where the time goes in v1:
time: 124 us
  Pallas kernels  121 us (98%)
  local copies, waits for them, and re-layouts  3.53 us (3%)
    pallas_call x1, Pallas kernels, shards(): pl.pallas_call(kernel, out_shape=jax.ShapeDtypeStruct((1, ROWS, COLS, D),...  121 us

profile of v1, /device:TPU:50, one launch (start us, length us, event | category | flops | bytes accessed | tf_op | source)
XLA Modules:
  0.0 124.2 jit_solution(2076736175528872397)
XLA Ops:
  0.0 1.3 %reshape.3.gain_ref = f32[1,1280]{1,0:T(1,128)} reshape(f32[1280]{0:T(1024)} %param.7) | data formatting | bytes 10240 | tf_op jit(solution)/shard_map/reshape | solution.py:292
  1.3 120.7 %window_attention.1 = bf16[1,10,40,1280]{3,2,1,0:T(8,128)(2,1)} custom-call(s32[4]{0:T(128)} %shift_ref.1, f32[1,1280]{1,0:T(1,128)} %reshape.3.gain_ref, bf16[1,10,40,1280]{3,2,1,0:T(8,128)(2,1)} %x_hbm.1, bf16[1280,1920]{1,0:T(8,128)(2,1)} %w_hbm.1, bf16[640,1280]{1,0:T(8,128)(2,1)} %wo_hbm.1), custom_call_target="tpu_custom_call" | custom-call | tf_op jit(solution)/shard_map/window_attention/pallas_call | solution.py:259
  122.0 2.2 %copy.7 = bf16[1,10,40,1280]{3,2,1,0:T(8,128)(2,1)} copy(bf16[1,10,40,1280]{3,2,1,0:T(8,128)(2,1)} %window_attention.1) | data formatting | bytes 2048000
